TPU v7x, 32 devices: a whole 2x2x4 slice. The times are simulated.
32 devices in a mesh: aux: 4 (over y, x), blk: 4 (over z), occ: 2 (over core).
Axes of the slice: x: 2, y: 2, z: 4, core: 2. Of those that a mesh axis runs over, the one named last changes fastest.
Arguments:
- integrals: bfloat16 [16, 4, 11, 512, 512], P('aux', 'blk'), may hold values from -0.078125 to 0.078125
- orbitals: bfloat16 [2048, 512], P('blk', 'occ'), may hold values from -6 to 6
- pair_lists: int32 [4, 11], P('blk'), may hold values from 0 to 3, as said below
- pair_counts: int32 [4], P('blk'), may hold values from 1 to 11, as said below
Outputs:
- exchange: float32 [4, 512, 512], P('blk', 'aux')
Inputs may be any that keep to these rules, and one draw needn't show every extreme that they name: `pair_lists`: entry 0 of row m is m itself; entries past pair_counts[m] are never read. `pair_counts`: some block has all 11 slots live.
All inputs are finite; a program needn't handle non-finite values.
Results may differ from a plain program's by a relative error of at most 0.00099.
Values may be sent and summed in bfloat16 or wider, within the bound.
No kernel may reach another device: no remote copies, remote signals or barrier semaphores. Data moves between devices by JAX's collectives and lax.ppermute only.
A program may use at most 192 MiB of HBM per device.

v0:
```python
import jax
import jax.numpy as jnp
from jax import lax
from jax.sharding import PartitionSpec as P


def slot_term(integral_block, picked):
    return jnp.einsum("pab,bi->pai", integral_block, picked, preferred_element_type=jnp.float32)


def zero_term(integral_block, picked):
    return jnp.zeros(
        (integral_block.shape[0], integral_block.shape[1], picked.shape[1]), jnp.float32
    )


def per_device(integrals, orbitals, pair_lists, pair_counts):
    local_ints = integrals[:, 0]
    width = orbitals.shape[0]
    columns = orbitals.shape[1]
    slot_total = pair_lists.shape[1]
    live = pair_counts[0]
    start_sum = jnp.zeros((local_ints.shape[0], width, columns), jnp.float32)
    carry = start_sum
    piece = lax.all_gather(orbitals, "blk", axis=0, tiled=True)
    piece_rows = piece.shape[0]
    for slot_index in range(slot_total):
        offset = pair_lists[0, slot_index] * width
        inside = (offset >= 0) & (offset < piece_rows) & (slot_index < live)
        picked = lax.dynamic_slice_in_dim(piece, jnp.clip(offset, 0, piece_rows - width), width, 0)
        carry = carry + lax.cond(inside, slot_term, zero_term, local_ints[:, slot_index], picked)
    halves = carry.astype(jnp.bfloat16)
    occ_total = columns * lax.axis_size("occ")
    partial_value = (
        jnp.einsum("pai,pbi->ab", halves, halves, preferred_element_type=jnp.float32) / occ_total
    )
    summed = lax.psum(partial_value, ("aux", "occ"))
    kept_rows = summed.shape[0] // lax.axis_size("aux")
    result = lax.dynamic_slice_in_dim(summed, lax.axis_index("aux") * kept_rows, kept_rows, 0)
    return result[None]


def solution(mesh):
    placed = (P("aux", "blk", None, None, None), P("blk", "occ"), P("blk", None), P("blk"))
    return jax.shard_map(
        per_device, mesh=mesh, in_specs=placed, out_specs=P("blk", "aux", None), check_vma=False
    )
```

profile of v0, /device:TPU:0, one launch (start us, length us, event | category | flops | bytes accessed | tf_op | source)
XLA Modules:
  0.0 163.6 jit_solution(8420829458339828189)
XLA Ops:
  6.5 0.0 all-gather.2.cloned.1.call-start
  6.5 1.8 %copy.5 = bf16[512,256]{0,1:T(8,128)(2,1)} copy(bf16[512,256]{1,0:T(8,128)(2,1)} %param.27) | data formatting | bytes 524288 | tf_op args[1]
  8.3 0.0 all-gather.2.cloned.1.call-update
  8.4 0.0 all-reduce.2.cloned.1.call-start
  8.4 1.7 %fusion.100 = (s32[1,1]{1,0:T(1,128)}, s32[1,1]{1,0:T(1,128)}, s32[1,1]{1,0:T(1,128)}, s32[1,1]{1,0:T(1,128)}, s32[1,1]{1,0:T(1,128)}, /*index=5*/s32[1,1]{1,0:T...) fusion(s32[1,11]{1,0:T(1,128)} %param.28), kind=kLoop, calls=%fused_computation.82 | loop fusion | bytes 88 | tf_op jit(solution)/shard_map/slice | solution.py:28
  17.7 20.0 %copy.12 = bf16[4,1,11,512,512]{4,3,0,2,1:T(8,128)(2,1)} copy(bf16[4,1,11,512,512]{4,3,2,1,0:T(8,128)(2,1)} %param.26) | data formatting | bytes 46137344 | tf_op args[0]
  37.6 2.0 %all-gather.2.cloned.1.call-done = bf16[2048,256]{0,1:T(8,128)(2,1)} async-done(((bf16[512,256]{0,1:T(8,128)(2,1)}), bf16[2048,256]{0,1:T(8,128)(2,1)}) %all-gather.2.cloned.1.call-update) | async-done | bytes 1048592 | tf_op jit(solution)/shard_map/all_gather | solution.py:25
  39.6 2.5 %conditional.11 = (f32[4,512,256]{1,2,0:T(8,128)S(1)}) conditional(s32[]{:T(128)} %convert_element_type.36, () %tuple.93, (s32[]{:T(128)}, bf16[2048,256]{0,1:T(8,128)(2,1)}, bf16[4,11,512,512]{3,2,0,1:T(8,128)(2,1)}) %tuple.151), branch_computations={%region_0.1_spmd, %region_1.2_spmd} | conditional | flops 536870912 | bytes 4456484 | solution.py:31
  39.6 2.5 %fusion.3 = f32[4,512,256]{1,2,0:T(8,128)S(1)} fusion(bf16[4,11,512,512]{3,2,0,1:T(8,128)(2,1)} %get-tuple-element.304, bf16[2048,256]{0,1:T(8,128)(2,1)} %get-tuple-element.302, s32[]{:T(128)S(6)} %min.45), kind=kOutput, calls=%fused_computation.3 | convolution fusion | flops 536870912 | bytes 4456452 | tf_op jit(solution)/shard_map/cond/branch_1_fun/pab,bi->pai/dot_general | solution.py:8
  42.1 3.9 %conditional.12 = (f32[4,512,256]{1,2,0:T(8,128)}) conditional(s32[]{:T(128)} %convert_element_type.37, () %tuple.95, (s32[]{:T(128)}, bf16[2048,256]{0,1:T(8,128)(2,1)}, bf16[4,11,512,512]{3,2,0,1:T(8,128)(2,1)}) %tuple.152), branch_computations={%region_2.3_spmd, %region_3.4_spmd} | conditional | flops 536870912 | bytes 4456484 | solution.py:31
  42.1 3.9 %fusion.12 = f32[4,512,256]{1,2,0:T(8,128)} fusion(bf16[4,11,512,512]{3,2,0,1:T(8,128)(2,1)} %get-tuple-element.307, bf16[2048,256]{0,1:T(8,128)(2,1)} %get-tuple-element.305, s32[]{:T(128)S(6)} %min.46), kind=kOutput, calls=%fused_computation.10 | convolution fusion | flops 536870912 | bytes 4456452 | tf_op jit(solution)/shard_map/cond/branch_1_fun/pab,bi->pai/dot_general | solution.py:8
  46.0 3.8 %conditional.13 = (f32[4,512,256]{1,2,0:T(8,128)}) conditional(s32[]{:T(128)} %convert_element_type.38, () %tuple.97, (s32[]{:T(128)}, bf16[2048,256]{0,1:T(8,128)(2,1)}, bf16[4,11,512,512]{3,2,0,1:T(8,128)(2,1)}) %tuple.153), branch_computations={%region_4.5_spmd, %region_5.6_spmd} | conditional | flops 536870912 | bytes 4456484 | solution.py:31
  46.0 3.8 %fusion.21 = f32[4,512,256]{1,2,0:T(8,128)} fusion(bf16[4,11,512,512]{3,2,0,1:T(8,128)(2,1)} %get-tuple-element.310, bf16[2048,256]{0,1:T(8,128)(2,1)} %get-tuple-element.308, s32[]{:T(128)S(6)} %min.47), kind=kOutput, calls=%fused_computation.17 | convolution fusion | flops 536870912 | bytes 4456452 | tf_op jit(solution)/shard_map/cond/branch_1_fun/pab,bi->pai/dot_general | solution.py:8
  49.9 3.8 %conditional.14 = (f32[4,512,256]{1,2,0:T(8,128)}) conditional(s32[]{:T(128)} %convert_element_type.39, () %tuple.99, (s32[]{:T(128)}, bf16[2048,256]{0,1:T(8,128)(2,1)}, bf16[4,11,512,512]{3,2,0,1:T(8,128)(2,1)}) %tuple.154), branch_computations={%region_6.7_spmd, %region_7.8_spmd} | conditional | flops 536870912 | bytes 4456484 | solution.py:31
  49.9 3.8 %fusion.30 = f32[4,512,256]{1,2,0:T(8,128)} fusion(bf16[4,11,512,512]{3,2,0,1:T(8,128)(2,1)} %get-tuple-element.313, bf16[2048,256]{0,1:T(8,128)(2,1)} %get-tuple-element.311, s32[]{:T(128)S(6)} %min.48), kind=kOutput, calls=%fused_computation.24 | convolution fusion | flops 536870912 | bytes 4456452 | tf_op jit(solution)/shard_map/cond/branch_1_fun/pab,bi->pai/dot_general | solution.py:8
  53.7 3.8 %conditional.15 = (f32[4,512,256]{1,2,0:T(8,128)}) conditional(s32[]{:T(128)} %convert_element_type.40, () %tuple.101, (s32[]{:T(128)}, bf16[2048,256]{0,1:T(8,128)(2,1)}, bf16[4,11,512,512]{3,2,0,1:T(8,128)(2,1)}) %tuple.155), branch_computations={%region_8.9_spmd, %region_9.10_spmd} | conditional | flops 536870912 | bytes 4456484 | solution.py:31
  53.7 3.8 %fusion.39 = f32[4,512,256]{1,2,0:T(8,128)} fusion(bf16[4,11,512,512]{3,2,0,1:T(8,128)(2,1)} %get-tuple-element.316, bf16[2048,256]{0,1:T(8,128)(2,1)} %get-tuple-element.314, s32[]{:T(128)S(6)} %min.49), kind=kOutput, calls=%fused_computation.31 | convolution fusion | flops 536870912 | bytes 4456452 | tf_op jit(solution)/shard_map/cond/branch_1_fun/pab,bi->pai/dot_general | solution.py:8
  57.4 3.8 %conditional.16 = (f32[4,512,256]{1,2,0:T(8,128)}) conditional(s32[]{:T(128)} %convert_element_type.41, () %tuple.103, (s32[]{:T(128)}, bf16[2048,256]{0,1:T(8,128)(2,1)}, bf16[4,11,512,512]{3,2,0,1:T(8,128)(2,1)}) %tuple.156), branch_computations={%region_10.11_spmd, %region_11.12_spmd} | conditional | flops 536870912 | bytes 4456484 | solution.py:31
  57.4 3.8 %fusion.48 = f32[4,512,256]{1,2,0:T(8,128)} fusion(bf16[4,11,512,512]{3,2,0,1:T(8,128)(2,1)} %get-tuple-element.319, bf16[2048,256]{0,1:T(8,128)(2,1)} %get-tuple-element.317, s32[]{:T(128)S(6)} %min.50), kind=kOutput, calls=%fused_computation.38 | convolution fusion | flops 536870912 | bytes 4456452 | tf_op jit(solution)/shard_map/cond/branch_1_fun/pab,bi->pai/dot_general | solution.py:8
  61.2 3.7 %conditional.17 = (f32[4,512,256]{1,2,0:T(8,128)}) conditional(s32[]{:T(128)} %convert_element_type.42, () %tuple.105, (s32[]{:T(128)}, bf16[2048,256]{0,1:T(8,128)(2,1)}, bf16[4,11,512,512]{3,2,0,1:T(8,128)(2,1)}) %tuple.157), branch_computations={%region_12.13_spmd, %region_13.14_spmd} | conditional | flops 536870912 | bytes 4456484 | solution.py:31
  61.2 3.7 %fusion.57 = f32[4,512,256]{1,2,0:T(8,128)} fusion(bf16[4,11,512,512]{3,2,0,1:T(8,128)(2,1)} %get-tuple-element.322, bf16[2048,256]{0,1:T(8,128)(2,1)} %get-tuple-element.320, s32[]{:T(128)S(6)} %min.51), kind=kOutput, calls=%fused_computation.45 | convolution fusion | flops 536870912 | bytes 4456452 | tf_op jit(solution)/shard_map/cond/branch_1_fun/pab,bi->pai/dot_general | solution.py:8
  65.0 3.8 %conditional.18 = (f32[4,512,256]{1,2,0:T(8,128)}) conditional(s32[]{:T(128)} %convert_element_type.43, () %tuple.107, (s32[]{:T(128)}, bf16[2048,256]{0,1:T(8,128)(2,1)}, bf16[4,11,512,512]{3,2,0,1:T(8,128)(2,1)}) %tuple.158), branch_computations={%region_14.15_spmd, %region_15.16_spmd} | conditional | flops 536870912 | bytes 4456484 | solution.py:31
  65.0 3.8 %fusion.66 = f32[4,512,256]{1,2,0:T(8,128)} fusion(bf16[4,11,512,512]{3,2,0,1:T(8,128)(2,1)} %get-tuple-element.325, bf16[2048,256]{0,1:T(8,128)(2,1)} %get-tuple-element.323, s32[]{:T(128)S(6)} %min.52), kind=kOutput, calls=%fused_computation.52 | convolution fusion | flops 536870912 | bytes 4456452 | tf_op jit(solution)/shard_map/cond/branch_1_fun/pab,bi->pai/dot_general | solution.py:8
  68.8 3.8 %conditional.19 = (f32[4,512,256]{1,2,0:T(8,128)}) conditional(s32[]{:T(128)} %convert_element_type.44, () %tuple.109, (s32[]{:T(128)}, bf16[2048,256]{0,1:T(8,128)(2,1)}, bf16[4,11,512,512]{3,2,0,1:T(8,128)(2,1)}) %tuple.159), branch_computations={%region_16.17_spmd, %region_17.18_spmd} | conditional | flops 536870912 | bytes 4456484 | solution.py:31
  68.8 3.8 %fusion.75 = f32[4,512,256]{1,2,0:T(8,128)} fusion(bf16[4,11,512,512]{3,2,0,1:T(8,128)(2,1)} %get-tuple-element.328, bf16[2048,256]{0,1:T(8,128)(2,1)} %get-tuple-element.326, s32[]{:T(128)S(6)} %min.53), kind=kOutput, calls=%fused_computation.59 | convolution fusion | flops 536870912 | bytes 4456452 | tf_op jit(solution)/shard_map/cond/branch_1_fun/pab,bi->pai/dot_general | solution.py:8
  72.6 3.8 %conditional.20 = (f32[4,512,256]{1,2,0:T(8,128)}) conditional(s32[]{:T(128)} %convert_element_type.45, () %tuple.111, (s32[]{:T(128)}, bf16[2048,256]{0,1:T(8,128)(2,1)}, bf16[4,11,512,512]{3,2,0,1:T(8,128)(2,1)}) %tuple.160), branch_computations={%region_18.19_spmd, %region_19.20_spmd} | conditional | flops 536870912 | bytes 4456484 | solution.py:31
  72.6 3.8 %fusion.84 = f32[4,512,256]{1,2,0:T(8,128)} fusion(bf16[4,11,512,512]{3,2,0,1:T(8,128)(2,1)} %get-tuple-element.331, bf16[2048,256]{0,1:T(8,128)(2,1)} %get-tuple-element.329, s32[]{:T(128)S(6)} %min.54), kind=kOutput, calls=%fused_computation.66 | convolution fusion | flops 536870912 | bytes 4456452 | tf_op jit(solution)/shard_map/cond/branch_1_fun/pab,bi->pai/dot_general | solution.py:8
  76.4 1.6 conditional.21
  76.4 1.6 broadcast.33
  78.0 18.2 %fusion.99 = f32[512,512]{1,0:T(8,128)} fusion(f32[4,512,256]{1,2,0:T(8,128)} %get-tuple-element.356, f32[4,512,256]{1,2,0:T(8,128)} %get-tuple-element.355, f32[4,512,256]{1,2,0:T(8,128)} %get-tuple-element.354, f32[4,512,256]{1,2,0:T(8,128)} %get-tuple-element.353, f32[4,512,256]{1,2,0:T(8,128)} %get-tuple-element.352, ...), kind=kOutput, calls=%fused_computation.80 | convolution fusion | flops 542900224 | bytes 24117248 | tf_op jit(solution)/shard_map/pai,pbi->ab/dot_general | solution.py:35
  96.2 0.0 all-reduce.2.cloned.1.call-update
  96.3 58.8 %all-reduce.2.cloned.1.call-done = f32[512,512]{1,0:T(8,128)} async-done(((f32[512,512]{1,0:T(8,128)}), f32[512,512]{1,0:T(8,128)}) %all-reduce.2.cloned.1.call-update) | async-done | bytes 1048592 | tf_op jit(solution)/shard_map/psum | solution.py:37
  155.0 1.7 %dynamic-slice_bitcast_fusion = f32[1,128,512]{2,1,0:T(8,128)} fusion(f32[512,512]{1,0:T(8,128)} %all-reduce.2.cloned.1.call-done, s32[]{:T(128)S(6)} %select_n.2), kind=kLoop, calls=%fused_computation.81 | loop fusion | bytes 524292 | tf_op jit(solution)/shard_map/broadcast_in_dim | solution.py:40
Async XLA Ops:
  6.5 33.1 %all-gather.2.cloned.1.call-start = ((), (), s32[]{:S(2)}) async-start(), calls=%async_computation | async-start | bytes 1310720 | tf_op jit(solution)/shard_map/all_gather | solution.py:25
  8.4 146.7 %all-reduce.2.cloned.1.call-start = ((), (), s32[]{:S(2)}) async-start(), calls=%async_computation.1 | async-start | bytes 2097152 | tf_op jit(solution)/shard_map/psum | solution.py:37
Sparse Core Ops, SparseCore 0:
  8.9 30.6 all-gather.1
  96.4 58.6 all-reduce.1
where the time goes:
time: 164 us
  waiting for transfers between devices  60.8 us (37%)
  matrix products  54.9 us (33%)
  local copies, waits for them, and re-layouts  26.8 us (16%)
  between operations  20.9 us (13%)
    psum x1, waiting for transfers between devices, per_device(): summed = lax.psum(partial_value, ('aux', 'occ'))  58.8 us
    dot_general x10, matrix products, slot_term(): jnp.einsum('pab,bi->pai', integral_block, picked, preferred_element_type=...  36.7 us
    unnamed x2, local copies, waits for them, and re-layouts  21.8 us
    dot_general x1, matrix products, per_device(): jnp.einsum('pai,pbi->ab', halves, halves, preferred_element_type=jnp.floa...  18.2 us
  transfers between devices with their start and end apart: 2, of which 2 were waited for; matrix products, arithmetic and copies ran while one was open for 13% of the time, Pallas kernels for 0%

commit v1 on v0

--- a/solution.py
+++ b/solution.py
@@ -34,7 +34,7 @@
     partial_value = (
         jnp.einsum("pai,pbi->ab", halves, halves, preferred_element_type=jnp.float32) / occ_total
     )
-    summed = lax.psum(partial_value, ("aux", "occ"))
+    summed = lax.psum(lax.psum(partial_value, "occ"), "aux")
     kept_rows = summed.shape[0] // lax.axis_size("aux")
     result = lax.dynamic_slice_in_dim(summed, lax.axis_index("aux") * kept_rows, kept_rows, 0)
     return result[None]

time: 164 us -> 184 us (1.12)
  waiting for transfers between devices: 60.8 us -> 80.3 us
    psum x1 -> x2, waiting for transfers between devices: 58.8 us -> 78.2 us  [per_device(): summed = lax.psum(lax.psum(partial_value, 'occ'), 'aux')]
  transfers between devices with their start and end apart: 2 -> 3, of which waited for: 2 -> 3; matrix products, arithmetic and copies ran while one was open for 13% -> 12% of each run, Pallas kernels for 0% -> 0%
where the time goes in v1:
time: 184 us; the launch traced here: 183 us
  waiting for transfers between devices  80.3 us (44%)
  matrix products  54.9 us (30%)
  local copies, waits for them, and re-layouts  26.8 us (15%)
  between operations  20.6 us (11%)
    psum x2, waiting for transfers between devices, per_device(): summed = lax.psum(lax.psum(partial_value, 'occ'), 'aux')  78.2 us
    dot_general x10, matrix products, slot_term(): jnp.einsum('pab,bi->pai', integral_block, picked, preferred_element_type=...  36.7 us
    unnamed x2, local copies, waits for them, and re-layouts  21.8 us
    dot_general x1, matrix products, per_device(): jnp.einsum('pai,pbi->ab', halves, halves, preferred_element_type=jnp.floa...  18.2 us
  transfers between devices with their start and end apart: 3, of which 3 were waited for; matrix products, arithmetic and copies ran while one was open for 12% of the time, Pallas kernels for 0%

profile of v1, /device:TPU:0, one launch (start us, length us, event | category | flops | bytes accessed | tf_op | source)
XLA Modules:
  0.0 182.7 jit_solution(13204741147665166352)
XLA Ops:
  6.5 0.0 all-gather.2.cloned.1.call-start
  6.5 1.8 copy.5
  8.3 0.0 all-gather.2.cloned.1.call-update
  8.4 0.0 all-reduce.3.cloned.1.call-start
  8.4 1.7 fusion.100
  17.7 20.0 %copy.12 = bf16[4,1,11,512,512]{4,3,0,2,1:T(8,128)(2,1)} copy(bf16[4,1,11,512,512]{4,3,2,1,0:T(8,128)(2,1)} %param.26) | data formatting | bytes 46137344 | tf_op args[0]
  37.6 2.0 %all-gather.2.cloned.1.call-done = bf16[2048,256]{0,1:T(8,128)(2,1)} async-done(((bf16[512,256]{0,1:T(8,128)(2,1)}), bf16[2048,256]{0,1:T(8,128)(2,1)}) %all-gather.2.cloned.1.call-update) | async-done | bytes 1048592 | tf_op jit(solution)/shard_map/all_gather | solution.py:25
  39.6 2.5 %conditional.11 = (f32[4,512,256]{1,2,0:T(8,128)S(1)}) conditional(s32[]{:T(128)} %convert_element_type.36, () %tuple.93, (s32[]{:T(128)}, bf16[2048,256]{0,1:T(8,128)(2,1)}, bf16[4,11,512,512]{3,2,0,1:T(8,128)(2,1)}) %tuple.153), branch_computations={%region_0.1_spmd, %region_1.2_spmd} | conditional | flops 536870912 | bytes 4456484 | solution.py:31
  39.6 2.5 %fusion.3 = f32[4,512,256]{1,2,0:T(8,128)S(1)} fusion(bf16[4,11,512,512]{3,2,0,1:T(8,128)(2,1)} %get-tuple-element.304, bf16[2048,256]{0,1:T(8,128)(2,1)} %get-tuple-element.302, s32[]{:T(128)S(6)} %min.45), kind=kOutput, calls=%fused_computation.3 | convolution fusion | flops 536870912 | bytes 4456452 | tf_op jit(solution)/shard_map/cond/branch_1_fun/pab,bi->pai/dot_general | solution.py:8
  42.1 3.9 %conditional.12 = (f32[4,512,256]{1,2,0:T(8,128)}) conditional(s32[]{:T(128)} %convert_element_type.37, () %tuple.95, (s32[]{:T(128)}, bf16[2048,256]{0,1:T(8,128)(2,1)}, bf16[4,11,512,512]{3,2,0,1:T(8,128)(2,1)}) %tuple.154), branch_computations={%region_2.3_spmd, %region_3.4_spmd} | conditional | flops 536870912 | bytes 4456484 | solution.py:31
  42.1 3.9 %fusion.12 = f32[4,512,256]{1,2,0:T(8,128)} fusion(bf16[4,11,512,512]{3,2,0,1:T(8,128)(2,1)} %get-tuple-element.307, bf16[2048,256]{0,1:T(8,128)(2,1)} %get-tuple-element.305, s32[]{:T(128)S(6)} %min.46), kind=kOutput, calls=%fused_computation.10 | convolution fusion | flops 536870912 | bytes 4456452 | tf_op jit(solution)/shard_map/cond/branch_1_fun/pab,bi->pai/dot_general | solution.py:8
  46.0 3.8 %conditional.13 = (f32[4,512,256]{1,2,0:T(8,128)}) conditional(s32[]{:T(128)} %convert_element_type.38, () %tuple.97, (s32[]{:T(128)}, bf16[2048,256]{0,1:T(8,128)(2,1)}, bf16[4,11,512,512]{3,2,0,1:T(8,128)(2,1)}) %tuple.155), branch_computations={%region_4.5_spmd, %region_5.6_spmd} | conditional | flops 536870912 | bytes 4456484 | solution.py:31
  46.0 3.8 %fusion.21 = f32[4,512,256]{1,2,0:T(8,128)} fusion(bf16[4,11,512,512]{3,2,0,1:T(8,128)(2,1)} %get-tuple-element.310, bf16[2048,256]{0,1:T(8,128)(2,1)} %get-tuple-element.308, s32[]{:T(128)S(6)} %min.47), kind=kOutput, calls=%fused_computation.17 | convolution fusion | flops 536870912 | bytes 4456452 | tf_op jit(solution)/shard_map/cond/branch_1_fun/pab,bi->pai/dot_general | solution.py:8
  49.9 3.8 %conditional.14 = (f32[4,512,256]{1,2,0:T(8,128)}) conditional(s32[]{:T(128)} %convert_element_type.39, () %tuple.99, (s32[]{:T(128)}, bf16[2048,256]{0,1:T(8,128)(2,1)}, bf16[4,11,512,512]{3,2,0,1:T(8,128)(2,1)}) %tuple.156), branch_computations={%region_6.7_spmd, %region_7.8_spmd} | conditional | flops 536870912 | bytes 4456484 | solution.py:31
  49.9 3.8 %fusion.30 = f32[4,512,256]{1,2,0:T(8,128)} fusion(bf16[4,11,512,512]{3,2,0,1:T(8,128)(2,1)} %get-tuple-element.313, bf16[2048,256]{0,1:T(8,128)(2,1)} %get-tuple-element.311, s32[]{:T(128)S(6)} %min.48), kind=kOutput, calls=%fused_computation.24 | convolution fusion | flops 536870912 | bytes 4456452 | tf_op jit(solution)/shard_map/cond/branch_1_fun/pab,bi->pai/dot_general | solution.py:8
  53.7 3.8 %conditional.15 = (f32[4,512,256]{1,2,0:T(8,128)}) conditional(s32[]{:T(128)} %convert_element_type.40, () %tuple.101, (s32[]{:T(128)}, bf16[2048,256]{0,1:T(8,128)(2,1)}, bf16[4,11,512,512]{3,2,0,1:T(8,128)(2,1)}) %tuple.157), branch_computations={%region_8.9_spmd, %region_9.10_spmd} | conditional | flops 536870912 | bytes 4456484 | solution.py:31
  53.7 3.8 %fusion.39 = f32[4,512,256]{1,2,0:T(8,128)} fusion(bf16[4,11,512,512]{3,2,0,1:T(8,128)(2,1)} %get-tuple-element.316, bf16[2048,256]{0,1:T(8,128)(2,1)} %get-tuple-element.314, s32[]{:T(128)S(6)} %min.49), kind=kOutput, calls=%fused_computation.31 | convolution fusion | flops 536870912 | bytes 4456452 | tf_op jit(solution)/shard_map/cond/branch_1_fun/pab,bi->pai/dot_general | solution.py:8
  57.4 3.8 %conditional.16 = (f32[4,512,256]{1,2,0:T(8,128)}) conditional(s32[]{:T(128)} %convert_element_type.41, () %tuple.103, (s32[]{:T(128)}, bf16[2048,256]{0,1:T(8,128)(2,1)}, bf16[4,11,512,512]{3,2,0,1:T(8,128)(2,1)}) %tuple.158), branch_computations={%region_10.11_spmd, %region_11.12_spmd} | conditional | flops 536870912 | bytes 4456484 | solution.py:31
  57.4 3.8 %fusion.48 = f32[4,512,256]{1,2,0:T(8,128)} fusion(bf16[4,11,512,512]{3,2,0,1:T(8,128)(2,1)} %get-tuple-element.319, bf16[2048,256]{0,1:T(8,128)(2,1)} %get-tuple-element.317, s32[]{:T(128)S(6)} %min.50), kind=kOutput, calls=%fused_computation.38 | convolution fusion | flops 536870912 | bytes 4456452 | tf_op jit(solution)/shard_map/cond/branch_1_fun/pab,bi->pai/dot_general | solution.py:8
  61.2 3.7 %conditional.17 = (f32[4,512,256]{1,2,0:T(8,128)}) conditional(s32[]{:T(128)} %convert_element_type.42, () %tuple.105, (s32[]{:T(128)}, bf16[2048,256]{0,1:T(8,128)(2,1)}, bf16[4,11,512,512]{3,2,0,1:T(8,128)(2,1)}) %tuple.159), branch_computations={%region_12.13_spmd, %region_13.14_spmd} | conditional | flops 536870912 | bytes 4456484 | solution.py:31
  61.2 3.7 %fusion.57 = f32[4,512,256]{1,2,0:T(8,128)} fusion(bf16[4,11,512,512]{3,2,0,1:T(8,128)(2,1)} %get-tuple-element.322, bf16[2048,256]{0,1:T(8,128)(2,1)} %get-tuple-element.320, s32[]{:T(128)S(6)} %min.51), kind=kOutput, calls=%fused_computation.45 | convolution fusion | flops 536870912 | bytes 4456452 | tf_op jit(solution)/shard_map/cond/branch_1_fun/pab,bi->pai/dot_general | solution.py:8
  65.0 3.8 %conditional.18 = (f32[4,512,256]{1,2,0:T(8,128)}) conditional(s32[]{:T(128)} %convert_element_type.43, () %tuple.107, (s32[]{:T(128)}, bf16[2048,256]{0,1:T(8,128)(2,1)}, bf16[4,11,512,512]{3,2,0,1:T(8,128)(2,1)}) %tuple.160), branch_computations={%region_14.15_spmd, %region_15.16_spmd} | conditional | flops 536870912 | bytes 4456484 | solution.py:31
  65.0 3.8 %fusion.66 = f32[4,512,256]{1,2,0:T(8,128)} fusion(bf16[4,11,512,512]{3,2,0,1:T(8,128)(2,1)} %get-tuple-element.325, bf16[2048,256]{0,1:T(8,128)(2,1)} %get-tuple-element.323, s32[]{:T(128)S(6)} %min.52), kind=kOutput, calls=%fused_computation.52 | convolution fusion | flops 536870912 | bytes 4456452 | tf_op jit(solution)/shard_map/cond/branch_1_fun/pab,bi->pai/dot_general | solution.py:8
  68.8 3.8 %conditional.19 = (f32[4,512,256]{1,2,0:T(8,128)}) conditional(s32[]{:T(128)} %convert_element_type.44, () %tuple.109, (s32[]{:T(128)}, bf16[2048,256]{0,1:T(8,128)(2,1)}, bf16[4,11,512,512]{3,2,0,1:T(8,128)(2,1)}) %tuple.161), branch_computations={%region_16.17_spmd, %region_17.18_spmd} | conditional | flops 536870912 | bytes 4456484 | solution.py:31
  68.8 3.8 %fusion.75 = f32[4,512,256]{1,2,0:T(8,128)} fusion(bf16[4,11,512,512]{3,2,0,1:T(8,128)(2,1)} %get-tuple-element.328, bf16[2048,256]{0,1:T(8,128)(2,1)} %get-tuple-element.326, s32[]{:T(128)S(6)} %min.53), kind=kOutput, calls=%fused_computation.59 | convolution fusion | flops 536870912 | bytes 4456452 | tf_op jit(solution)/shard_map/cond/branch_1_fun/pab,bi->pai/dot_general | solution.py:8
  72.6 3.8 %conditional.20 = (f32[4,512,256]{1,2,0:T(8,128)}) conditional(s32[]{:T(128)} %convert_element_type.45, () %tuple.111, (s32[]{:T(128)}, bf16[2048,256]{0,1:T(8,128)(2,1)}, bf16[4,11,512,512]{3,2,0,1:T(8,128)(2,1)}) %tuple.162), branch_computations={%region_18.19_spmd, %region_19.20_spmd} | conditional | flops 536870912 | bytes 4456484 | solution.py:31
  72.6 3.8 %fusion.84 = f32[4,512,256]{1,2,0:T(8,128)} fusion(bf16[4,11,512,512]{3,2,0,1:T(8,128)(2,1)} %get-tuple-element.331, bf16[2048,256]{0,1:T(8,128)(2,1)} %get-tuple-element.329, s32[]{:T(128)S(6)} %min.54), kind=kOutput, calls=%fused_computation.66 | convolution fusion | flops 536870912 | bytes 4456452 | tf_op jit(solution)/shard_map/cond/branch_1_fun/pab,bi->pai/dot_general | solution.py:8
  76.4 1.6 conditional.21
  76.4 1.6 broadcast.33
  78.0 18.2 %fusion.99 = f32[512,512]{1,0:T(8,128)} fusion(f32[4,512,256]{1,2,0:T(8,128)} %get-tuple-element.356, f32[4,512,256]{1,2,0:T(8,128)} %get-tuple-element.355, f32[4,512,256]{1,2,0:T(8,128)} %get-tuple-element.354, f32[4,512,256]{1,2,0:T(8,128)} %get-tuple-element.353, f32[4,512,256]{1,2,0:T(8,128)} %get-tuple-element.352, ...), kind=kOutput, calls=%fused_computation.80 | convolution fusion | flops 542900224 | bytes 24117248 | tf_op jit(solution)/shard_map/pai,pbi->ab/dot_general | solution.py:35
  96.2 0.0 all-reduce.3.cloned.1.call-update
  96.3 0.0 all-reduce.5.cloned.1.call-start
  96.3 21.5 %all-reduce.3.cloned.1.call-done = f32[512,512]{1,0:T(8,128)} async-done(((f32[512,512]{1,0:T(8,128)}), f32[512,512]{1,0:T(8,128)}) %all-reduce.3.cloned.1.call-update) | async-done | bytes 1048592 | tf_op jit(solution)/shard_map/psum | solution.py:37
  117.8 0.0 all-reduce.5.cloned.1.call-update
  117.8 56.7 %all-reduce.5.cloned.1.call-done = f32[512,512]{1,0:T(8,128)} async-done(((f32[512,512]{1,0:T(8,128)}), f32[512,512]{1,0:T(8,128)}) %all-reduce.5.cloned.1.call-update) | async-done | bytes 1048592 | tf_op jit(solution)/shard_map/psum | solution.py:37
  174.5 1.7 dynamic-slice_bitcast_fusion
Async XLA Ops:
  6.5 33.1 %all-gather.2.cloned.1.call-start = ((), (), s32[]{:S(2)}) async-start(), calls=%async_computation | async-start | bytes 1310720 | tf_op jit(solution)/shard_map/all_gather | solution.py:25
  8.4 109.4 %all-reduce.3.cloned.1.call-start = ((), (), s32[]{:S(2)}) async-start(), calls=%async_computation.1 | async-start | bytes 2097152 | tf_op jit(solution)/shard_map/psum | solution.py:37
  96.3 78.3 %all-reduce.5.cloned.1.call-start = ((), (), s32[]{:S(2)}) async-start(), calls=%async_computation.2 | async-start | bytes 2097152 | tf_op jit(solution)/shard_map/psum | solution.py:37
Sparse Core Ops, SparseCore 0:
  8.9 30.6 all-gather.1
  96.4 21.3 all-reduce.2
  120.9 53.6 all-reduce.4
